TPU v7x, 32 devices: a whole 2x2x4 slice. The times are simulated.
32 devices in a mesh: sx: 8 (over y, x, core), sy: 4 (over z).
Axes of the slice: x: 2, y: 2, z: 4, core: 2. Of those that a mesh axis runs over, the one named last changes fastest.
Arguments:
- coeffs: float32 [2, 8, 16, 4, 128, 128], P(None, 'sx', None, 'sy'), may hold values from -6 to 6
- deform: float32 [2, 4], replicated, may hold values from -0.08 to 0.08
Outputs:
- spectrum: float32 [2, 128, 512, 128], P(None, 'sx', 'sy')
All inputs are finite; a program needn't handle non-finite values.
Results may differ from a plain program's by a relative error of at most 0.0014.
Values sent between devices are 32-bit elements; how exact they have to be, the bound alone decides.
A program may use at most 64 MiB of HBM per device.

v0:
```python
import functools
import math

import jax
import jax.numpy as jnp
import numpy as np
from jax import lax
from jax.experimental import pallas as pl
from jax.experimental.pallas import tpu as pltpu
from jax.sharding import PartitionSpec as P

NODES = 4
RHS = 8
ROWS = 8
MESH = pl.DeviceIdType.MESH


def cheb_nodes(count):
    return (1.0 - np.cos(np.pi * (2.0 * np.arange(count) + 1.0) / (2.0 * count))) / 2.0


def lagrange_table(count):
    nodes = cheb_nodes(count)
    table = np.ones((count, 2, count))
    for row in range(count):
        for sibling in range(2):
            spots = (sibling + nodes) / 2.0
            for other in range(count):
                if other != row:
                    table[row, sibling] *= (spots - nodes[other]) / (nodes[row] - nodes[other])
    return table


def mix_matrix(along, right_sides, count):
    table = lagrange_table(count)
    blocks = []
    for sibling in range(2):
        weights = table[:, sibling].T
        eye = np.eye(count)
        inner = np.kron(weights, eye) if along == 0 else np.kron(eye, weights)
        blocks.append(np.kron(np.eye(right_sides), inner))
    return (np.concatenate(blocks, axis=0) * math.sqrt(0.5)).astype(np.float32)


TAYLOR_SIN = [((-1.0) ** k) * (2.0 * math.pi) ** (2 * k + 1) / math.factorial(2 * k + 1) for k in range(8)]
TAYLOR_COS = [((-1.0) ** k) * (2.0 * math.pi) ** (2 * k) / math.factorial(2 * k) for k in range(8)]


def horner(coefs, u):
    acc = coefs[-1] * u + coefs[-2]
    for c in coefs[-3::-1]:
        acc = acc * u + c
    return acc


def turns(t):
    half = jnp.floor(2.0 * t + 0.5)
    rest = t - 0.5 * half
    parity = half - 2.0 * jnp.floor(0.5 * half)
    sign = 1.0 - 2.0 * parity
    u = rest * rest
    return sign * horner(TAYLOR_COS, u), sign * rest * horner(TAYLOR_SIN, u)


def split_index(value, by):
    return lax.div(value, by), lax.rem(value, by)


def plan_of(space_x, space_y):
    steps = []
    sx, sy, row = space_x, space_y, 0
    while sx > 1 or sy > 1:
        if sx > 1:
            steps.append((0, sx, sy, row))
            row += max(8, sx * sy)
            sx //= 2
        if sy > 1:
            steps.append((1, sx, sy, row))
            row += max(8, sx * sy)
            sy //= 2
    return steps, row


def kernel(
    dims,
    deform_ref,
    nodes_ref,
    mix_ref,
    coeffs_ref,
    out_ref,
    recv,
    twid,
    base1,
    base2,
    last1,
    last2,
    lhs,
    state,
    send_sem,
    recv_sem,
):
    space_x, space_y, local_x, local_y, rows, modes = dims
    steps, _ = plan_of(space_x, space_y)
    chunks_y = local_y // rows
    chunks = local_x * chunks_y
    boxes = space_x * space_y
    gain_x, gain_y = space_x, space_y
    mx = lax.axis_index("sx")
    my = lax.axis_index("sy")
    me = mx * space_y + my

    barrier = pltpu.get_barrier_semaphore()

    def peer_of(i):
        ox, oy = split_index(i, space_y)
        return lax.rem(mx + ox, space_x), lax.rem(my + oy, space_y)

    def greet(i, _):
        px, py = peer_of(i)
        pl.semaphore_signal(barrier, inc=1, device_id=(px, py), device_id_type=MESH)
        return 0

    lax.fori_loop(1, boxes, greet, 0)

    node_x = nodes_ref[0:1, :]
    node_y = nodes_ref[1:2, :]

    def warped(sx, sy, count):
        box = lax.broadcasted_iota(jnp.int32, (count, 128), 0)
        ax = (box // sy).astype(jnp.float32)
        ay = (box % sy).astype(jnp.float32)
        p1 = (ax + node_x) / sx
        p2 = (ay + node_y) / sy
        y1, y2 = 0.0, 0.0
        for m in range(modes):
            y1 = y1 + deform_ref[0, m] * turns((p1 + p2) * (0.5 * (m + 1)))[1]
            y2 = y2 + deform_ref[1, m] * turns((p1 - p2) * (0.5 * (m + 1)))[1]
        return p1 + y1, p2 + y2

    for along, sx, sy, row in steps[1:]:
        count = max(8, sx * sy)
        y1, y2 = warped(sx, sy, count)
        c, s = turns((y1 * (0.25 * sx)) if along == 0 else (y2 * (0.25 * sy)))
        twid[0, pl.ds(row, count), :] = c
        twid[1, pl.ds(row, count), :] = s

    y1, y2 = warped(space_x, space_y, boxes)
    for fx in range(local_x):
        for child in range(2):
            freq = (mx * local_x + fx).astype(jnp.float32) + (0.25 + 0.5 * child)
            c, s = turns(y1 * (freq * gain_x))
            base1[0, 2 * fx + child] = c
            base1[1, 2 * fx + child] = s
    twid[0, pl.ds(0, boxes), :] = y2

    def base_box(i, _):
        freq = lax.broadcasted_iota(jnp.int32, (local_y, 128), 0) + my * local_y
        warp = twid[0, pl.ds(i, 1), :]
        c, s = turns(warp * ((freq.astype(jnp.float32) + 0.5) * gain_y))
        base2[0, i] = c
        base2[1, i] = s
        return 0

    lax.fori_loop(0, boxes, base_box, 0)

    y1, y2 = warped(1, 1, 8)
    out_x = local_x * space_x
    freq = lax.broadcasted_iota(jnp.int32, (out_x, 128), 0) + mx * out_x
    c, s = turns(y1[0:1] * (freq.astype(jnp.float32) + 0.5))
    last1[0] = c
    last1[1] = s
    for child in range(space_y):
        freq = (lax.broadcasted_iota(jnp.int32, (local_y, 128), 0) + my * local_y) * space_y + child
        c, s = turns(y2[0:1] * (freq.astype(jnp.float32) + 0.5))
        last2[0, child] = c
        last2[1, child] = s

    pl.semaphore_wait(barrier, boxes - 1)

    def piece(k, px, py):
        fx, fy = split_index(k, chunks_y)
        start = pl.multiple_of(py * local_y + fy * rows, 8)
        return coeffs_ref.at[:, 0, px * local_x + fx, 0, pl.ds(start, rows), :]

    def send_chunk(k, _):
        def send(i, _):
            px, py = peer_of(i)
            pltpu.make_async_remote_copy(
                src_ref=piece(k, px, py),
                dst_ref=recv.at[k, me],
                send_sem=send_sem.at[k],
                recv_sem=recv_sem.at[k],
                device_id=(px, py),
                device_id_type=MESH,
            ).start()
            return 0

        lax.fori_loop(1, boxes, send, 0)
        pltpu.make_async_copy(piece(k, mx, my), recv.at[k, me], recv_sem.at[k]).start()
        return 0

    lax.fori_loop(0, chunks, send_chunk, 0)

    def rotate_into(slot, pair, sibling, size, re0, im0, re1, im1):
        lanes = pl.ds(128 * sibling, 128)
        base = pair * 4 * size
        lhs[slot, pl.ds(base, size), lanes] = re0
        lhs[slot, pl.ds(base + size, size), lanes] = im0
        lhs[slot, pl.ds(base + 2 * size, size), lanes] = re1
        lhs[slot, pl.ds(base + 3 * size, size), lanes] = im1

    def pair_of(along, sy, a1, a2):
        if along == 0:
            return (a1 // 2) * sy + a2, a1 % 2
        return a1 * (sy // 2) + a2 // 2, a2 % 2

    def compute(k, _):
        pltpu.make_async_copy(recv.at[k], recv.at[k], recv_sem.at[k]).wait()
        fx, fy = split_index(k, chunks_y)
        fy_rows = pl.ds(pl.multiple_of(fy * rows, 8), rows)
        size = rows
        for number, (along, sx, sy, row) in enumerate(steps):
            slot = number % 2
            for a1 in range(sx):
                for a2 in range(sy):
                    box = a1 * sy + a2
                    pair, sibling = pair_of(along, sy, a1, a2)
                    if number == 0:
                        re, im = recv[k, box, 0], recv[k, box, 1]
                        c, s = base2[0, box, fy_rows, :], base2[1, box, fy_rows, :]
                        re, im = re * c + im * s, im * c - re * s
                        c, s = base1[0, 2 * fx, pl.ds(box, 1), :], base1[1, 2 * fx, pl.ds(box, 1), :]
                        re0, im0 = re * c + im * s, im * c - re * s
                        c, s = base1[0, 2 * fx + 1, pl.ds(box, 1), :], base1[1, 2 * fx + 1, pl.ds(box, 1), :]
                        re1, im1 = re * c + im * s, im * c - re * s
                    else:
                        at = box * 2 * size
                        half = size // 2
                        re = jnp.concatenate(
                            [state[pl.ds(at, half), :], state[pl.ds(at + 2 * half, half), :]], axis=0
                        )
                        im = jnp.concatenate(
                            [state[pl.ds(at + half, half), :], state[pl.ds(at + 3 * half, half), :]], axis=0
                        )
                        c, s = twid[0, pl.ds(row + box, 1), :], twid[1, pl.ds(row + box, 1), :]
                        rc, rs, ic, js = re * c, re * s, im * c, im * s
                        re0, im0 = rc - js, ic + rs
                        re1, im1 = rc + js, ic - rs
                    rotate_into(slot, pair, sibling, size, re0, im0, re1, im1)
            state[...] = jnp.dot(
                lhs[slot], mix_ref[along], precision=lax.Precision.HIGHEST, preferred_element_type=jnp.float32
            )
            size *= 2
        total = len(steps)
        for code in range(1 << total):
            bits = [(code >> n) & 1 for n in range(total)]
            at = 0
            for n in range(total - 1):
                at += bits[n] * rows * (1 << n)
            half = rows * (1 << (total - 1))
            at += bits[total - 1] * 2 * half
            bx, by = 0, 0
            for n, (along, _, _, _) in enumerate(steps):
                if along == 0:
                    bx = 2 * bx + bits[n]
                else:
                    by = 2 * by + bits[n]
            re = state[pl.ds(at, rows), :]
            im = state[pl.ds(at + half, rows), :]
            first = fx * space_x + bx
            c1, s1 = last1[0, pl.ds(first, 1), :], last1[1, pl.ds(first, 1), :]
            c2, s2 = last2[0, by, fy_rows, :], last2[1, by, fy_rows, :]
            c = c1 * c2 - s1 * s2
            s = s1 * c2 + c1 * s2
            spots = pl.ds(fy * (rows * space_y) + by, rows, stride=space_y)
            out_ref[0, first, spots, :] = re * c - im * s
            out_ref[1, first, spots, :] = im * c + re * s
        return 0

    lax.fori_loop(0, chunks, compute, 0)

    def drain(k, _):
        sent = recv.at[k, pl.ds(0, boxes - 1)]
        pltpu.make_async_copy(sent, sent, send_sem.at[k]).wait()
        return 0

    lax.fori_loop(0, chunks, drain, 0)


def body(coeffs, deform):
    space_x, space_y = lax.axis_size("sx"), lax.axis_size("sy")
    _, _, freq_x, _, freq_y, lanes = coeffs.shape
    local_x, local_y = freq_x // space_x, freq_y // space_y
    rows = ROWS
    chunks = local_x * local_y // rows
    boxes = space_x * space_y
    out_x, out_y = local_x * space_x, local_y * space_y
    lane_ids = np.arange(lanes)
    table = cheb_nodes(NODES)
    nodes = jnp.asarray(
        np.stack([table[lane_ids // NODES % NODES], table[lane_ids % NODES]]), dtype=jnp.float32
    )
    right_sides = lanes // NODES**2
    mix = jnp.asarray(np.stack([mix_matrix(0, right_sides, NODES), mix_matrix(1, right_sides, NODES)]))
    _, twid_rows = plan_of(space_x, space_y)
    dims = (space_x, space_y, local_x, local_y, rows, deform.shape[1])
    vmem = pl.BlockSpec(memory_space=pltpu.VMEM)
    state_rows = boxes * 2 * rows
    f32 = jnp.float32
    return pl.pallas_call(
        functools.partial(kernel, dims),
        out_shape=jax.ShapeDtypeStruct((2, out_x, out_y, lanes), f32),
        in_specs=[
            pl.BlockSpec(memory_space=pltpu.SMEM),
            vmem,
            vmem,
            pl.BlockSpec(memory_space=pl.ANY),
        ],
        out_specs=vmem,
        scratch_shapes=[
            pltpu.VMEM((chunks, boxes, 2, rows, lanes), f32),
            pltpu.VMEM((2, twid_rows, lanes), f32),
            pltpu.VMEM((2, 2 * local_x, boxes, lanes), f32),
            pltpu.VMEM((2, boxes, local_y, lanes), f32),
            pltpu.VMEM((2, out_x, lanes), f32),
            pltpu.VMEM((2, space_y, local_y, lanes), f32),
            pltpu.VMEM((2, state_rows, 2 * lanes), f32),
            pltpu.VMEM((state_rows, lanes), f32),
            pltpu.SemaphoreType.DMA((chunks,)),
            pltpu.SemaphoreType.DMA((chunks,)),
        ],
        compiler_params=pltpu.CompilerParams(collective_id=0, has_side_effects=True),
        name="butterfly",
    )(deform, nodes, mix, coeffs)


def solution(mesh):
    placed = (P(None, "sx", None, "sy", None, None), P())
    return jax.shard_map(
        body, mesh=mesh, in_specs=placed, out_specs=P(None, "sx", "sy", None), check_vma=False
    )
```

profile of v0, /device:TPU:0, one launch (start us, length us, event | category | flops | bytes accessed | tf_op | source)
XLA Modules:
  0.0 67.8 jit_solution(12382724217450576933)
XLA Ops:
  0.0 64.7 %butterfly.1 = f32[2,16,128,128]{3,2,1,0:T(8,128)} custom-call(f32[2,4]{1,0:T(2,128)} %deform_ref.1, f32[2,128]{1,0:T(2,128)} %constant.4.clone.nodes_ref, f32[2,256,128]{2,1,0:T(8,128)} %constant.5.clone.mix_ref, f32[2,1,16,1,128,128]{5,4,3,2,1,0:T(8,128)} %coeffs_ref.1), custom_call_target="tpu_custom_call" | custom-call | tf_op jit(solution)/shard_map/butterfly/pallas_call | solution.py:310
  64.7 3.1 %copy.6 = f32[2,16,128,128]{3,2,1,0:T(8,128)} copy(f32[2,16,128,128]{3,2,1,0:T(8,128)} %butterfly.1) | data formatting | bytes 4194304
where the time goes:
time: 68.2 us; the launch traced here: 67.8 us
  Pallas kernels  64.7 us (95%)
  local copies, waits for them, and re-layouts  3.14 us (5%)
    pallas_call x1, Pallas kernels, body(): pl.pallas_call(functools.partial(kernel, dims), out_shape=jax.ShapeDtypeS...  64.7 us
    unnamed x1, local copies, waits for them, and re-layouts  3.14 us

commit v1 on v0

--- a/solution.py
+++ b/solution.py
@@ -94,7 +94,8 @@
     base2,
     last1,
     last2,
-    lhs,
+    lhs_high,
+    lhs_low,
     state,
     send_sem,
     recv_sem,
@@ -112,8 +113,8 @@
     barrier = pltpu.get_barrier_semaphore()
 
     def peer_of(i):
-        ox, oy = split_index(i, space_y)
-        return lax.rem(mx + ox, space_x), lax.rem(my + oy, space_y)
+        oy, ox = split_index(i, space_x)
+        return lax.rem(mx + ox, space_x), lax.rem(my + space_y - oy, space_y)
 
     def greet(i, _):
         px, py = peer_of(i)
@@ -184,7 +185,7 @@
 
     def send_chunk(k, _):
         def send(i, _):
-            px, py = peer_of(i)
+            px, py = peer_of(boxes - i)
             pltpu.make_async_remote_copy(
                 src_ref=piece(k, px, py),
                 dst_ref=recv.at[k, me],
@@ -202,12 +203,11 @@
     lax.fori_loop(0, chunks, send_chunk, 0)
 
     def rotate_into(slot, pair, sibling, size, re0, im0, re1, im1):
-        lanes = pl.ds(128 * sibling, 128)
-        base = pair * 4 * size
-        lhs[slot, pl.ds(base, size), lanes] = re0
-        lhs[slot, pl.ds(base + size, size), lanes] = im0
-        lhs[slot, pl.ds(base + 2 * size, size), lanes] = re1
-        lhs[slot, pl.ds(base + 3 * size, size), lanes] = im1
+        spot = (slot, pl.ds(pair * 4 * size, 4 * size), pl.ds(128 * sibling, 128))
+        whole = jnp.concatenate([re0, im0, re1, im1], axis=0)
+        high = whole.astype(jnp.bfloat16)
+        lhs_high[spot] = high
+        lhs_low[spot] = (whole - high.astype(jnp.float32)).astype(jnp.bfloat16)
 
     def pair_of(along, sy, a1, a2):
         if along == 0:
@@ -247,9 +247,9 @@
                         re0, im0 = rc - js, ic + rs
                         re1, im1 = rc + js, ic - rs
                     rotate_into(slot, pair, sibling, size, re0, im0, re1, im1)
-            state[...] = jnp.dot(
-                lhs[slot], mix_ref[along], precision=lax.Precision.HIGHEST, preferred_element_type=jnp.float32
-            )
+            by_high = jnp.dot(lhs_high[slot], mix_ref[along], preferred_element_type=jnp.float32)
+            by_low = jnp.dot(lhs_low[slot], mix_ref[along, :, 0:128], preferred_element_type=jnp.float32)
+            state[...] = by_high[:, 0:128] + (by_high[:, 128:256] + by_low)
             size *= 2
         total = len(steps)
         for code in range(1 << total):
@@ -301,7 +301,10 @@
         np.stack([table[lane_ids // NODES % NODES], table[lane_ids % NODES]]), dtype=jnp.float32
     )
     right_sides = lanes // NODES**2
-    mix = jnp.asarray(np.stack([mix_matrix(0, right_sides, NODES), mix_matrix(1, right_sides, NODES)]))
+    mix = np.stack([mix_matrix(0, right_sides, NODES), mix_matrix(1, right_sides, NODES)])
+    high = mix.astype(jnp.bfloat16)
+    low = (mix - high.astype(np.float32)).astype(jnp.bfloat16)
+    mix = jnp.asarray(np.concatenate([high, low], axis=2))
     _, twid_rows = plan_of(space_x, space_y)
     dims = (space_x, space_y, local_x, local_y, rows, deform.shape[1])
     vmem = pl.BlockSpec(memory_space=pltpu.VMEM)
@@ -309,7 +312,7 @@
     f32 = jnp.float32
     return pl.pallas_call(
         functools.partial(kernel, dims),
-        out_shape=jax.ShapeDtypeStruct((2, out_x, out_y, lanes), f32),
+        out_shape=pltpu.VMEM((2, out_x, out_y, lanes), f32),
         in_specs=[
             pl.BlockSpec(memory_space=pltpu.SMEM),
             vmem,
@@ -324,7 +327,8 @@
             pltpu.VMEM((2, boxes, local_y, lanes), f32),
             pltpu.VMEM((2, out_x, lanes), f32),
             pltpu.VMEM((2, space_y, local_y, lanes), f32),
-            pltpu.VMEM((2, state_rows, 2 * lanes), f32),
+            pltpu.VMEM((2, state_rows, 2 * lanes), jnp.bfloat16),
+            pltpu.VMEM((2, state_rows, 2 * lanes), jnp.bfloat16),
             pltpu.VMEM((state_rows, lanes), f32),
             pltpu.SemaphoreType.DMA((chunks,)),
             pltpu.SemaphoreType.DMA((chunks,)),

time: 68.2 us -> 57.2 us (0.84)
  Pallas kernels: 64.7 us -> 55.7 us
  local copies, waits for them, and re-layouts: 3.14 us -> 1.32 us
    pallas_call x1, Pallas kernels: 64.7 us -> 55.7 us  [body(): pl.pallas_call(functools.partial(kernel, dims), out_shape=pltpu.VMEM((2,...]
    unnamed x1, local copies, waits for them, and re-layouts: 3.14 us -> 1.32 us
where the time goes in v1:
time: 57.2 us; the launch traced here: 57 us
  Pallas kernels  55.7 us (97%)
  local copies, waits for them, and re-layouts  1.32 us (2%)
    pallas_call x1, Pallas kernels, body(): pl.pallas_call(functools.partial(kernel, dims), out_shape=pltpu.VMEM((2,...  55.7 us
    unnamed x1, local copies, waits for them, and re-layouts  1.32 us

profile of v1, /device:TPU:0, one launch (start us, length us, event | category | flops | bytes accessed | tf_op | source)
XLA Modules:
  0.0 57.0 jit_solution(14194180692703965779)
XLA Ops:
  0.0 55.7 %butterfly.1 = f32[2,16,128,128]{3,2,1,0:T(8,128)S(1)} custom-call(f32[2,4]{1,0:T(2,128)} %deform_ref.1, f32[2,128]{1,0:T(2,128)} %constant.4.clone.nodes_ref, bf16[2,256,256]{2,1,0:T(8,128)(2,1)} %constant.5.clone.mix_ref, f32[2,1,16,1,128,128]{5,4,3,2,1,0:T(8,128)} %coeffs_ref.1), custom_call_target="tpu_custom_call" | custom-call | tf_op jit(solution)/shard_map/butterfly/pallas_call | solution.py:313
  55.7 1.3 %copy.6 = f32[2,16,128,128]{3,2,1,0:T(8,128)} copy(f32[2,16,128,128]{3,2,1,0:T(8,128)S(1)} %butterfly.1) | data formatting | bytes 4194304

commit v2 on v1

--- a/solution.py
+++ b/solution.py
@@ -83,9 +83,8 @@
 
 def kernel(
     dims,
-    deform_ref,
-    nodes_ref,
-    mix_ref,
+    deform_hbm,
+    mix_hbm,
     coeffs_ref,
     out_ref,
     recv,
@@ -99,6 +98,11 @@
     state,
     send_sem,
     recv_sem,
+    deform_ref,
+    mix_ref,
+    deform_sem,
+    mix_sem,
+    plane_sem,
 ):
     space_x, space_y, local_x, local_y, rows, modes = dims
     steps, _ = plan_of(space_x, space_y)
@@ -112,19 +116,31 @@
 
     barrier = pltpu.get_barrier_semaphore()
 
-    def peer_of(i):
-        oy, ox = split_index(i, space_x)
-        return lax.rem(mx + ox, space_x), lax.rem(my + space_y - oy, space_y)
-
-    def greet(i, _):
-        px, py = peer_of(i)
-        pl.semaphore_signal(barrier, inc=1, device_id=(px, py), device_id_type=MESH)
-        return 0
-
-    lax.fori_loop(1, boxes, greet, 0)
-
-    node_x = nodes_ref[0:1, :]
-    node_y = nodes_ref[1:2, :]
+    for o in range(1, space_y):
+        pl.semaphore_signal(
+            barrier, inc=1, device_id=(mx, lax.rem(my + o, space_y)), device_id_type=MESH
+        )
+    for o in range(1, space_x):
+        pl.semaphore_signal(
+            barrier, inc=1, device_id=(lax.rem(mx + o, space_x), my), device_id_type=MESH
+        )
+    fetch_mix = pltpu.make_async_copy(mix_hbm, mix_ref, mix_sem)
+    fetch_mix.start()
+    fetch_deform = pltpu.make_async_copy(deform_hbm, deform_ref, deform_sem)
+    fetch_deform.start()
+    fetch_deform.wait()
+
+    lane = lax.broadcasted_iota(jnp.int32, (1, 128), 1)
+    spots = [float(q) for q in cheb_nodes(NODES)]
+
+    def node_of(index):
+        node = jnp.full((1, 128), spots[0], jnp.float32)
+        for t in range(1, NODES):
+            node = jnp.where(index == t, spots[t], node)
+        return node
+
+    node_x = node_of(lane // NODES % NODES)
+    node_y = node_of(lane % NODES)
 
     def warped(sx, sy, count):
         box = lax.broadcasted_iota(jnp.int32, (count, 128), 0)
@@ -176,31 +192,47 @@
         last2[0, child] = c
         last2[1, child] = s
 
-    pl.semaphore_wait(barrier, boxes - 1)
-
     def piece(k, px, py):
         fx, fy = split_index(k, chunks_y)
         start = pl.multiple_of(py * local_y + fy * rows, 8)
         return coeffs_ref.at[:, 0, px * local_x + fx, 0, pl.ds(start, rows), :]
 
+    def send(k, px, py):
+        pltpu.make_async_remote_copy(
+            src_ref=piece(k, px, py),
+            dst_ref=recv.at[k, me],
+            send_sem=send_sem.at[k],
+            recv_sem=recv_sem.at[k],
+            device_id=(px, py),
+            device_id_type=MESH,
+        ).start()
+
+    pl.semaphore_wait(barrier, space_x + space_y - 2)
+    for o in range(1, space_x):
+        pl.semaphore_signal(
+            plane_sem, inc=1, device_id=(lax.rem(mx + o, space_x), my), device_id_type=MESH
+        )
+
+    def send_line(k, _):
+        for o in range(1, space_y):
+            send(k, mx, lax.rem(my + o, space_y))
+        return 0
+
+    lax.fori_loop(0, chunks, send_line, 0)
+    pl.semaphore_wait(plane_sem, space_x - 1)
+
     def send_chunk(k, _):
-        def send(i, _):
-            px, py = peer_of(boxes - i)
-            pltpu.make_async_remote_copy(
-                src_ref=piece(k, px, py),
-                dst_ref=recv.at[k, me],
-                send_sem=send_sem.at[k],
-                recv_sem=recv_sem.at[k],
-                device_id=(px, py),
-                device_id_type=MESH,
-            ).start()
+        def send_one(i, _):
+            oy, ox = split_index(i, space_x - 1)
+            send(k, lax.rem(mx + 1 + ox, space_x), lax.rem(my + 1 + oy, space_y))
             return 0
 
-        lax.fori_loop(1, boxes, send, 0)
+        lax.fori_loop(0, boxes - space_y, send_one, 0)
         pltpu.make_async_copy(piece(k, mx, my), recv.at[k, me], recv_sem.at[k]).start()
         return 0
 
     lax.fori_loop(0, chunks, send_chunk, 0)
+    fetch_mix.wait()
 
     def rotate_into(slot, pair, sibling, size, re0, im0, re1, im1):
         spot = (slot, pl.ds(pair * 4 * size, 4 * size), pl.ds(128 * sibling, 128))
@@ -295,11 +327,6 @@
     chunks = local_x * local_y // rows
     boxes = space_x * space_y
     out_x, out_y = local_x * space_x, local_y * space_y
-    lane_ids = np.arange(lanes)
-    table = cheb_nodes(NODES)
-    nodes = jnp.asarray(
-        np.stack([table[lane_ids // NODES % NODES], table[lane_ids % NODES]]), dtype=jnp.float32
-    )
     right_sides = lanes // NODES**2
     mix = np.stack([mix_matrix(0, right_sides, NODES), mix_matrix(1, right_sides, NODES)])
     high = mix.astype(jnp.bfloat16)
@@ -314,9 +341,8 @@
         functools.partial(kernel, dims),
         out_shape=pltpu.VMEM((2, out_x, out_y, lanes), f32),
         in_specs=[
-            pl.BlockSpec(memory_space=pltpu.SMEM),
-            vmem,
-            vmem,
+            pl.BlockSpec(memory_space=pl.ANY),
+            pl.BlockSpec(memory_space=pl.ANY),
             pl.BlockSpec(memory_space=pl.ANY),
         ],
         out_specs=vmem,
@@ -332,10 +358,15 @@
             pltpu.VMEM((state_rows, lanes), f32),
             pltpu.SemaphoreType.DMA((chunks,)),
             pltpu.SemaphoreType.DMA((chunks,)),
+            pltpu.SMEM(deform.shape, f32),
+            pltpu.VMEM(mix.shape, mix.dtype),
+            pltpu.SemaphoreType.DMA,
+            pltpu.SemaphoreType.DMA,
+            pltpu.SemaphoreType.REGULAR,
         ],
         compiler_params=pltpu.CompilerParams(collective_id=0, has_side_effects=True),
         name="butterfly",
-    )(deform, nodes, mix, coeffs)
+    )(deform, mix, coeffs)
 
 
 def solution(mesh):

time: 57.2 us -> 56 us (0.979)
  Pallas kernels: 55.7 us -> 54.5 us
    pallas_call x1, Pallas kernels: 55.7 us -> 54.5 us  [body(): pl.pallas_call(functools.partial(kernel, dims), out_shape=pltpu.VMEM((2,...]
where the time goes in v2:
time: 56 us; the launch traced here: 55.8 us
  Pallas kernels  54.5 us (97%)
  local copies, waits for them, and re-layouts  1.32 us (2%)
    pallas_call x1, Pallas kernels, body(): pl.pallas_call(functools.partial(kernel, dims), out_shape=pltpu.VMEM((2,...  54.5 us
    unnamed x1, local copies, waits for them, and re-layouts  1.32 us

profile of v2, /device:TPU:0, one launch (start us, length us, event | category | flops | bytes accessed | tf_op | source)
XLA Modules:
  0.0 55.8 jit_solution(8084181189911083427)
XLA Ops:
  0.0 54.5 %butterfly.1 = f32[2,16,128,128]{3,2,1,0:T(8,128)S(1)} custom-call(f32[2,4]{1,0:T(2,128)} %deform_hbm.1, bf16[2,256,256]{2,1,0:T(8,128)(2,1)} %constant.2.clone.mix_hbm, f32[2,1,16,1,128,128]{5,4,3,2,1,0:T(8,128)} %coeffs_ref.1), custom_call_target="tpu_custom_call" | custom-call | tf_op jit(solution)/shard_map/butterfly/pallas_call | solution.py:340
  54.5 1.3 %copy.5 = f32[2,16,128,128]{3,2,1,0:T(8,128)} copy(f32[2,16,128,128]{3,2,1,0:T(8,128)S(1)} %butterfly.1) | data formatting | bytes 4194304
